TPU v7x, 256 devices: a whole 4x4x8 slice. The times are simulated.
256 devices in a mesh: expert: 64 (over y, z, core), tensor: 4 (over x).
Axes of the slice: x: 4, y: 4, z: 8, core: 2. Of those that a mesh axis runs over, the one named last changes fastest.
Arguments:
- activations: bfloat16 [32768, 4096], P(('expert', 'tensor')), may hold values from -6 to 6
- out_grad: bfloat16 [32768, 4096], P(('expert', 'tensor')), may hold values from -6 to 6
- expert_ids: int32 [32768, 1], P('expert'), may hold values from 0 to 63; in each aligned block of 128 rows (0 to 127, 128 to 255, ...) at most 3 rows name the same one
- gate_weights: bfloat16 [32768, 1], P('expert'), may hold values from 0.049804688 to 1
- weight_in: bfloat16 [64, 4096, 1536], P('expert', None, 'tensor'), may hold values from -0.09375 to 0.09375
- weight_out: bfloat16 [64, 1536, 4096], P('expert', 'tensor'), may hold values from -0.15625 to 0.15625
Outputs:
- grad_in: bfloat16 [32768, 4096], P(('expert', 'tensor'))
- grad_gates: float32 [32768, 1], P(('expert', 'tensor'))
- grad_weight_out: bfloat16 [64, 1536, 4096], P('expert', 'tensor')
Inputs may be any that keep to these rules, and one draw needn't show every extreme that they name: `expert_ids`: each token names 1 different experts. Among the 128 tokens of one device (aligned blocks of rows) no expert is named by more than 3 tokens, and in every draw some expert is named by exactly 3 tokens of some device.
All inputs are finite; a program needn't handle non-finite values.
Results may differ from a plain program's by a relative error of at most 0.013.
Values may be sent and summed in bfloat16 or wider, within the bound.
No kernel may reach another device: no remote copies, remote signals or barrier semaphores. Data moves between devices by JAX's collectives and lax.ppermute only.
A program may use at most 128 MiB of HBM per device.

v0:
```python
import functools

import jax
import jax.numpy as jnp
from jax import lax
from jax.experimental import pallas as pl
from jax.experimental.pallas import tpu as pltpu
from jax.sharding import PartitionSpec as P

EXPERTS = 64
CAP = 3
ROOT_HALF = 0.7071067811865476
INV_ROOT_TAU = 0.3989422804014327


def slot_positions(expert_ids):
    rows = expert_ids.shape[0]
    same = expert_ids[:, None] == expert_ids[None, :]
    before = jnp.arange(rows)[None, :] < jnp.arange(rows)[:, None]
    return jnp.sum((same & before).astype(jnp.int32), axis=1)


def shift(value, step):
    size = lax.axis_size("tensor")
    return lax.ppermute(value, "tensor", [(i, (i + step) % size) for i in range(size)])


def ring_gather(upper, lower):
    left_u, right_l = shift(upper, 1), shift(lower, -1)
    left_l, right_u = shift(lower, 1), shift(upper, -1)
    far_u, far_l = shift(left_u, 1), shift(right_l, -1)
    return (upper, lower, left_u, left_l, right_u, right_l, far_u, far_l), (left_u, right_l, left_l, right_u)


def after(value, *others):
    return lax.optimization_barrier((value, others))[0]


HBM = pl.BlockSpec(memory_space=pltpu.HBM)
PARAMS = pltpu.CompilerParams(vmem_limit_bytes=60 << 20)
TRANSPOSED = (((1,), (1,)), ((), ()))


def start_all(copies):
    for copy in copies:
        copy.start()


def wait_all(copies):
    for copy in copies:
        copy.wait()


def expert_kernel(begin, count, *refs):
    place, tokens, grads = refs[0], refs[1], refs[2 : 2 + count]
    w_in, w_out, activated_ref = refs[2 + count : 5 + count]
    partials = refs[5 + count : 9 + count]
    rows, grad_rows, w_in_v, w_out_v, result, sems, grad_sems, out_sems = refs[9 + count :]
    piece, width = grads[0].shape
    n = piece * count // 4
    block = tokens.shape[0] // 4
    me = place[0]
    owners = (me, lax.rem(me + 3, 4), lax.rem(me + 1, 4), lax.rem(me + 2, 4))
    first = [pltpu.make_async_copy(w_in, w_in_v, sems.at[4])]
    for i in range(4):
        start = pl.multiple_of(owners[i] * block + begin, 64)
        first.append(pltpu.make_async_copy(tokens.at[pl.ds(start, n)], rows.at[pl.ds(i * n, n)], sems.at[i]))
    second = [pltpu.make_async_copy(w_out, w_out_v, sems.at[5])]
    for i in range(count):
        target = grad_rows.at[pl.ds(i * piece, piece)]
        second.append(pltpu.make_async_copy(grads[i], target, grad_sems.at[i]))
    start_all(first + second)
    wait_all(first)
    pre = jnp.dot(rows[...], w_in_v[...], preferred_element_type=jnp.float32)
    cdf = 0.5 * (1.0 + lax.erf(pre * ROOT_HALF))
    slope = cdf + pre * INV_ROOT_TAU * jnp.exp(-0.5 * pre * pre)
    activated = (pre * cdf).astype(jnp.bfloat16)
    activated_ref[...] = activated
    wait_all(second)
    grad = lax.dot_general(grad_rows[...], w_out_v[...], TRANSPOSED, preferred_element_type=jnp.float32)
    score = jnp.sum(activated.astype(jnp.float32) * grad, axis=1, keepdims=True)
    result[:, width:] = jnp.broadcast_to(score, (4 * n, 128)).astype(jnp.bfloat16)
    grad_pre = (grad * slope).astype(jnp.bfloat16)
    stores = []
    for pair in (1, 0):
        rows_of = slice(pair * 2 * n, (pair + 1) * 2 * n)
        part = lax.dot_general(grad_pre[rows_of], w_in_v[...], TRANSPOSED, preferred_element_type=jnp.float32)
        result[rows_of, :width] = part.astype(jnp.bfloat16)
        for i in (2 * pair, 2 * pair + 1):
            stores.append(pltpu.make_async_copy(result.at[pl.ds(i * n, n)], partials[i], out_sems.at[i]))
            stores[-1].start()
    wait_all(stores)


def expert_math(begin, place, tokens, grads, w_in, w_out):
    count, (piece, width) = len(grads), grads[0].shape
    n = piece * count // 4
    hidden = w_in.shape[1]
    bf16 = jnp.bfloat16
    outs = pl.pallas_call(
        functools.partial(expert_kernel, begin, count),
        out_shape=[jax.ShapeDtypeStruct((4 * n, hidden), bf16)]
        + [jax.ShapeDtypeStruct((n, width + 128), bf16)] * 4,
        in_specs=[pl.BlockSpec(memory_space=pltpu.SMEM)] + [HBM] * (3 + count),
        out_specs=[pl.BlockSpec(memory_space=pltpu.VMEM)] + [HBM] * 4,
        scratch_shapes=[
            pltpu.VMEM((4 * n, width), bf16),
            pltpu.VMEM((4 * n, width), bf16),
            pltpu.VMEM(w_in.shape, bf16),
            pltpu.VMEM(w_out.shape, bf16),
            pltpu.VMEM((4 * n, width + 128), bf16),
            pltpu.SemaphoreType.DMA((6,)),
            pltpu.SemaphoreType.DMA((8,)),
            pltpu.SemaphoreType.DMA((4,)),
        ],
        compiler_params=PARAMS,
        name="expert",
    )(place, tokens, *grads, w_in, w_out)
    return outs[0], outs[1:]


def weight_grad_kernel(counts, *refs):
    parts = len(counts)
    acts, grads = refs[0:parts], refs[parts : parts + sum(counts)]
    out, act_rows, grad_rows, a_sems, g_sems = refs[parts + sum(counts) :]
    block = act_rows.shape[0] // 4

    @pl.when(pl.program_id(0) == 0)
    def _():
        copies, begin, number = [], 0, 0
        for k in range(parts):
            n = acts[k].shape[0] // 4
            for i in range(4):
                target = act_rows.at[pl.ds(i * block + begin, n)]
                copies.append(pltpu.make_async_copy(acts[k].at[pl.ds(i * n, n)], target, a_sems.at[4 * k + i]))
            each = counts[k] // 4
            for i in range(counts[k]):
                piece = n // each
                target = grad_rows.at[pl.ds(i // each * block + begin + i % each * piece, piece)]
                copies.append(pltpu.make_async_copy(grads[number + i], target, g_sems.at[number + i]))
            begin, number = begin + n, number + counts[k]
        start_all(copies)
        wait_all(copies)

    columns = out.shape[1]
    start = pl.multiple_of(pl.program_id(0) * columns, columns)
    out[...] = lax.dot_general(
        act_rows[...],
        grad_rows[:, pl.ds(start, columns)],
        (((0,), (0,)), ((), ())),
        preferred_element_type=jnp.float32,
    ).astype(jnp.bfloat16)


def weight_grad(acts, grads):
    hidden, width = acts[0].shape[1], grads[0][0].shape[1]
    rows = sum(act.shape[0] for act in acts)
    counts = tuple(len(pieces) for pieces in grads)
    bf16 = jnp.bfloat16
    return pl.pallas_call(
        functools.partial(weight_grad_kernel, counts),
        grid=(8,),
        out_shape=jax.ShapeDtypeStruct((hidden, width), bf16),
        in_specs=[HBM] * (len(acts) + sum(counts)),
        out_specs=pl.BlockSpec((hidden, width // 8), lambda i: (0, i)),
        scratch_shapes=[
            pltpu.VMEM((rows, hidden), bf16),
            pltpu.VMEM((rows, width), bf16),
            pltpu.SemaphoreType.DMA((4 * len(acts),)),
            pltpu.SemaphoreType.DMA((sum(counts),)),
        ],
        compiler_params=PARAMS,
        name="weight_grad",
    )(*acts, *[piece for pieces in grads for piece in pieces])


def on_device(activations, out_grad, expert_ids, gate_weights, weight_in, weight_out):
    rows, width = activations.shape
    experts = lax.axis_size("expert")
    blocks = width // 128
    first = lax.axis_index("tensor") * rows
    ids = lax.dynamic_slice_in_dim(expert_ids[:, 0], first, rows)
    gates = lax.dynamic_slice_in_dim(gate_weights[:, 0], first, rows).astype(jnp.float32)
    slots = ids * CAP + slot_positions(ids)
    table = (slots[:, None] == jnp.arange(EXPERTS * CAP, dtype=jnp.int32)).astype(jnp.bfloat16)
    scaled = (gates[:, None] * out_grad.astype(jnp.float32)).astype(jnp.bfloat16)
    w_in, w_out = weight_in[0], weight_out[0]

    def exchange(value):
        return lax.all_to_all(value, "expert", split_axis=0, concat_axis=0, tiled=True)

    def pack(values):
        packed = jnp.dot(table.T, values, preferred_element_type=jnp.float32)
        return packed.astype(jnp.bfloat16).reshape(experts, CAP * blocks, 128)

    def by_slot(there, k):
        return there[:, k * blocks : (k + 1) * blocks].reshape(experts, width)

    packed, sent = lax.optimization_barrier((pack(activations), pack(scaled)))
    last = sent[:, (CAP - 1) * blocks :]
    early = (last, shift(last, 1), shift(last, -1), shift(last, 2))
    there = exchange(packed)
    mine = after(jnp.concatenate([by_slot(there, k) for k in range(CAP)], axis=0), early)
    tokens = lax.all_gather(mine, "tensor", axis=0, tiled=True)
    there = exchange(after(sent[:, : (CAP - 1) * blocks], early, there))
    whole = exchange(after(jnp.concatenate(early, axis=1), there))
    ring, _ = ring_gather(by_slot(there, 0), by_slot(there, 1))
    grads = [ring]
    place = lax.axis_index("tensor").reshape(1)
    acts, parts, sums = [], [], []
    for turn in range(2):
        begin = turn * (CAP - 1) * experts
        if turn == 1:
            grads.append(tuple(by_slot(after(whole, acts[0]), i) for i in range(4)))
        activated, (own, left, right, far) = expert_math(begin, place, tokens, grads[turn], w_in, w_out)
        acts.append(activated)
        parts.append([own, shift(far, 2), shift(left, -1), shift(right, 1)])
    parts[0] = after(parts[0], acts[1])
    for turn in range(2):
        if turn == 1:
            pair = jnp.concatenate([sums[0][:experts, :width], sums[0][experts:, :width]], axis=1)
            back = exchange(pair.reshape(experts, 2 * blocks, 128))
        sums.append(sum(part.astype(jnp.float32) for part in parts[turn]).astype(jnp.bfloat16))
    slotwise = [sums[0][:experts], sums[0][experts:], sums[1]]
    rest = [sums[1][:, :width]] + [part[:, width:] for part in slotwise]
    rest, acts[0], back = lax.optimization_barrier((jnp.concatenate(rest, axis=1), acts[0], back))
    rest = exchange(rest.reshape(experts, -1, 128)).reshape(experts, -1)
    back = back.reshape(experts, 2 * width)
    backs = [back[:, :width], back[:, width:], rest[:, :width]]
    chosen = [rest[:, width + 128 * k : width + 128 * (k + 1)] for k in range(CAP)]
    grad_w_out = weight_grad(acts, grads)
    spreads = [(slots[:, None] == jnp.arange(EXPERTS) * CAP + k).astype(jnp.bfloat16) for k in range(CAP)]
    grad_in = sum(jnp.dot(spreads[k], backs[k], preferred_element_type=jnp.float32) for k in range(CAP))
    chosen = sum(jnp.dot(spreads[k], chosen[k], preferred_element_type=jnp.float32) for k in range(CAP))
    grad_gates = (chosen[:, 0] / gates)[:, None]
    return (grad_in.astype(jnp.bfloat16), grad_gates, grad_w_out[None])


def solution(mesh):
    return jax.shard_map(
        on_device,
        mesh=mesh,
        in_specs=(
            P(("expert", "tensor"), None),
            P(("expert", "tensor"), None),
            P("expert", None),
            P("expert", None),
            P("expert", None, "tensor"),
            P("expert", "tensor", None),
        ),
        out_specs=(
            P(("expert", "tensor"), None),
            P(("expert", "tensor"), None),
            P("expert", "tensor", None),
        ),
        check_vma=False,
    )
```

profile of v0, /device:TPU:1, one launch (start us, length us, event | category | flops | bytes accessed | tf_op | source)
XLA Modules:
  0.0 313.1 jit_solution(16701607339096795328)
XLA Ops:
  7.2 0.7 fusion.35
  8.1 0.7 fusion.34
  8.8 0.7 convolution_convert_fusion.1
  9.5 2.1 reshape.71
  11.6 0.7 convolution_convert_fusion
  12.3 0.8 reshape.72
  13.1 13.2 %all-to-all-start = ((bf16[64,96,128]{2,1,0:T(8,128)(2,1)}), bf16[64,96,128]{2,1,0:T(8,128)(2,1)S(1)}, u32[]{:S(2)}, u32[]{:S(2)}) async-start(bf16[64,96,128]{2,1,0:T(8,128)(2,1)} %reshape.71), calls=%async_computation | async-start | bytes 3145728 | tf_op jit(solution)/shard_map/all_to_all | solution.py:190
  26.3 0.9 slice.79
  27.2 1.2 collective-permute-start
  28.4 1.5 collective-permute-start.1
  29.8 1.5 collective-permute-start.2
  31.4 34.7 %all-to-all-done = bf16[64,96,128]{2,1,0:T(8,128)(2,1)S(1)} async-done(((bf16[64,96,128]{2,1,0:T(8,128)(2,1)}), bf16[64,96,128]{2,1,0:T(8,128)(2,1)S(1)}, u32[]{:S(2)}, u32[]{:S(2)}) %all-to-all-start) | async-done | bytes 1572896 | tf_op jit(solution)/shard_map/all_to_all | solution.py:190
  66.0 0.3 fusion.37
  66.3 0.4 copy_bitcast_fusion.8
  66.7 0.2 copy.40
  66.9 1.3 pad_maximum_fusion.1
  68.3 1.1 slice.80
  69.4 6.1 %all-to-all-start.1 = ((bf16[64,64,128]{2,1,0:T(8,128)(2,1)}), bf16[64,64,128]{2,1,0:T(8,128)(2,1)S(1)}, u32[]{:S(2)}, u32[]{:S(2)}) async-start(bf16[64,64,128]{2,1,0:T(8,128)(2,1)} %slice.80), calls=%async_computation.1 | async-start | bytes 2097152 | tf_op jit(solution)/shard_map/all_to_all | solution.py:190
  75.5 3.3 %pad_maximum_fusion = bf16[64,128,128]{2,1,0:T(8,128)(2,1)} fusion(bf16[64,32,128]{2,1,0:T(8,128)(2,1)} %collective-permute-done.2, bf16[64,32,128]{2,1,0:T(8,128)(2,1)} %collective-permute-done.1, bf16[64,32,128]{2,1,0:T(8,128)(2,1)} %collective-permute-done, bf16[64,32,128]{2,1,0:T(8,128)(2,1)} %slice.79), kind=kLoop, calls=%fused_computation.6 | loop fusion | flops 8388608 | bytes 4194304 | tf_op jit(solution)/shard_map/concatenate | solution.py:206
  78.8 25.2 %all-to-all-done.1 = bf16[64,64,128]{2,1,0:T(8,128)(2,1)S(1)} async-done(((bf16[64,64,128]{2,1,0:T(8,128)(2,1)}), bf16[64,64,128]{2,1,0:T(8,128)(2,1)S(1)}, u32[]{:S(2)}, u32[]{:S(2)}) %all-to-all-start.1) | async-done | bytes 1048608 | tf_op jit(solution)/shard_map/all_to_all | solution.py:190
  104.1 6.2 %all-to-all-start.2 = ((bf16[64,128,128]{2,1,0:T(8,128)(2,1)}), bf16[64,128,128]{2,1,0:T(8,128)(2,1)S(1)}, u32[]{:S(2)}, u32[]{:S(2)}) async-start(bf16[64,128,128]{2,1,0:T(8,128)(2,1)} %pad_maximum_fusion), calls=%async_computation.2 | async-start | bytes 4194304 | tf_op jit(solution)/shard_map/all_to_all | solution.py:190
  110.6 0.2 copy.38
  110.8 1.3 collective-permute-start.3
  112.1 1.5 collective-permute-start.6
  113.6 2.7 collective-permute-start.5
  116.2 20.8 %collective-permute-done.3.refs_4_ = bf16[64,4096]{1,0:T(8,128)(2,1)S(1)} collective-permute-done((bf16[64,4096]{1,0:T(8,128)(2,1)S(1)}, bf16[64,4096]{1,0:T(8,128)(2,1)S(1)}, u32[]{:S(2)}, u32[]{:S(2)}) %collective-permute-start.3) | collective-permute-done | bytes 524320 | tf_op jit(solution)/shard_map/ppermute | solution.py:25
  137.1 2.7 collective-permute-start.8
  139.7 15.7 %collective-permute-done.4.refs_5_ = bf16[64,4096]{1,0:T(8,128)(2,1)S(1)} collective-permute-done((bf16[64,4096]{1,0:T(8,128)(2,1)S(1)}, bf16[64,4096]{1,0:T(8,128)(2,1)S(1)}, u32[]{:S(2)}, u32[]{:S(2)}) %collective-permute-start.4) | collective-permute-done | bytes 524320 | tf_op jit(solution)/shard_map/ppermute | solution.py:25
  155.5 11.2 %collective-permute-done.7.refs_8_ = bf16[64,4096]{1,0:T(8,128)(2,1)S(1)} collective-permute-done((bf16[64,4096]{1,0:T(8,128)(2,1)S(1)}, bf16[64,4096]{1,0:T(8,128)(2,1)S(1)}, u32[]{:S(2)}, u32[]{:S(2)}) %collective-permute-start.7) | collective-permute-done | bytes 524320 | tf_op jit(solution)/shard_map/ppermute | solution.py:25
  166.7 0.8 copy-done.8
  167.5 13.5 %expert.2 = (bf16[512,384]{1,0:T(8,128)(2,1)}, bf16[128,4224]{1,0:T(8,128)(2,1)}, bf16[128,4224]{1,0:T(8,128)(2,1)}, bf16[128,4224]{1,0:T(8,128)(2,1)}, bf16[128,4224]{1,0:T(8,128)(2,1)}) custom-call(s32[1]{0:T(128)} %bitcast.3.refs_0_, bf16[768,4096]{1,0:T(8,128)(2,1)} %all-gather.2.cloned.1.call-done.refs_1_, bf16[64,4096]{1,0:T(8,128)(2,1)} %bitcast.66, ...), custom_call_target="tpu_custom_call" | custom-call | tf_op jit(solution)/shard_map/expert/pallas_call | solution.py:100
  181.1 1.4 collective-permute-start.12
  182.4 1.2 collective-permute-start.13
  183.6 0.3 collective-permute-start.14
  183.9 0.4 fusion.36
  184.3 1.0 copy.37
  185.3 1.0 copy.36
  186.3 1.0 copy.35
  187.4 1.0 copy.34
  188.4 9.3 %expert.3 = (bf16[256,384]{1,0:T(8,128)(2,1)}, bf16[64,4224]{1,0:T(8,128)(2,1)}, bf16[64,4224]{1,0:T(8,128)(2,1)}, bf16[64,4224]{1,0:T(8,128)(2,1)}, bf16[64,4224]{1,0:T(8,128)(2,1)}) custom-call(s32[1]{0:T(128)} %bitcast.3.refs_0_, bf16[768,4096]{1,0:T(8,128)(2,1)} %all-gather.2.cloned.1.call-done.refs_1_, bf16[64,4096]{1,0:T(8,128)(2,1)} %bitcast.72, ...), custom_call_target="tpu_custom_call" | custom-call | tf_op jit(solution)/shard_map/expert/pallas_call | solution.py:100
  197.7 2.6 collective-permute-start.10
  200.4 7.2 %collective-permute-done.12 = bf16[128,4224]{1,0:T(8,128)(2,1)S(1)} collective-permute-done((bf16[128,4224]{1,0:T(8,128)(2,1)}, bf16[128,4224]{1,0:T(8,128)(2,1)S(1)}, u32[]{:S(2)}, u32[]{:S(2)}) %collective-permute-start.12) | collective-permute-done | bytes 1081376 | tf_op jit(solution)/shard_map/ppermute | solution.py:25
  207.6 1.2 collective-permute-start.9
  208.8 20.5 %collective-permute-done.13 = bf16[128,4224]{1,0:T(8,128)(2,1)} collective-permute-done((bf16[128,4224]{1,0:T(8,128)(2,1)}, bf16[128,4224]{1,0:T(8,128)(2,1)}, u32[]{:S(2)}, u32[]{:S(2)}) %collective-permute-start.13) | collective-permute-done | bytes 1081376 | tf_op jit(solution)/shard_map/ppermute | solution.py:25
  229.3 2.6 collective-permute-done.14
  231.9 2.1 add_convert_fusion
  234.2 1.3 copy.18
  235.5 10.6 %all-to-all-start.3 = ((bf16[64,64,128]{2,1,0:T(8,128)(2,1)}), bf16[64,64,128]{2,1,0:T(8,128)(2,1)S(1)}, u32[]{:S(2)}, u32[]{:S(2)}) async-start(bf16[64,64,128]{2,1,0:T(8,128)(2,1)} %bitcast.27), calls=%async_computation.3 | async-start | bytes 2097152 | tf_op jit(solution)/shard_map/all_to_all | solution.py:190
  246.1 7.9 %collective-permute-done.9 = bf16[64,4224]{1,0:T(8,128)(2,1)} collective-permute-done((bf16[64,4224]{1,0:T(8,128)(2,1)}, bf16[64,4224]{1,0:T(8,128)(2,1)}, u32[]{:S(2)}, u32[]{:S(2)}) %collective-permute-start.9) | collective-permute-done | bytes 540704 | tf_op jit(solution)/shard_map/ppermute | solution.py:25
  254.1 1.6 add_convert_fusion.1
  255.8 18.8 %all-to-all-done.3 = bf16[64,64,128]{2,1,0:T(8,128)(2,1)S(1)} async-done(((bf16[64,64,128]{2,1,0:T(8,128)(2,1)}), bf16[64,64,128]{2,1,0:T(8,128)(2,1)S(1)}, u32[]{:S(2)}, u32[]{:S(2)}) %all-to-all-start.3) | async-done | bytes 1048608 | tf_op jit(solution)/shard_map/all_to_all | solution.py:190
  274.7 1.1 reshape.84
  275.8 6.4 %all-to-all-start.4 = ((bf16[64,35,128]{2,1,0:T(8,128)(2,1)}), bf16[64,35,128]{2,1,0:T(8,128)(2,1)}, u32[]{:S(2)}, u32[]{:S(2)}) async-start(bf16[64,35,128]{2,1,0:T(8,128)(2,1)} %reshape.84), calls=%async_computation.4 | async-start | bytes 1310720 | tf_op jit(solution)/shard_map/all_to_all | solution.py:190
  282.2 0.7 copy.32
  282.9 8.7 %weight_grad.1 = bf16[384,4096]{1,0:T(8,128)(2,1)} custom-call(bf16[512,384]{1,0:T(8,128)(2,1)} %get-tuple-element.48.refs_0_, bf16[256,384]{1,0:T(8,128)(2,1)} %get-tuple-element.41.refs_1_, bf16[64,4096]{1,0:T(8,128)(2,1)} %bitcast.67, bf16[64,4096]{1,0:T(8,128)(2,1)} %bitcast.71, bf16[64,4096]{1,0:T(8,128)(2,1)} %copy-done.4, bf16[64,4096]{1,0:T(8,128)(2,1)} %copy-done.6, ...), custom_call_target="tpu_custom_call" | custom-call | tf_op jit(solution)/shard_map/weight_grad/pallas_call | solution.py:160
  291.6 0.5 fusion.4
  292.1 0.5 convolution_add_fusion.1
  292.6 9.7 %all-to-all-done.4 = bf16[64,35,128]{2,1,0:T(8,128)(2,1)} async-done(((bf16[64,35,128]{2,1,0:T(8,128)(2,1)}), bf16[64,35,128]{2,1,0:T(8,128)(2,1)}, u32[]{:S(2)}, u32[]{:S(2)}) %all-to-all-start.4) | async-done | bytes 573472 | tf_op jit(solution)/shard_map/all_to_all | solution.py:190
  302.2 1.3 copy.33
  303.5 0.2 fusion.9
  303.7 0.2 fusion.12
  304.0 0.2 fusion.6
  304.2 1.5 fusion
  305.7 0.5 fusion.33
  (53 shorter events, 1.0 us)
Async XLA Ops:
  7.2 1.6 copy-start
  9.5 2.1 copy-start.12
  9.5 2.1 copy-start.10
  13.1 53.0 %all-to-all-start = ((bf16[64,96,128]{2,1,0:T(8,128)(2,1)}), bf16[64,96,128]{2,1,0:T(8,128)(2,1)S(1)}, u32[]{:S(2)}, u32[]{:S(2)}) async-start(bf16[64,96,128]{2,1,0:T(8,128)(2,1)} %reshape.71), calls=%async_computation | async-start | bytes 3145728 | tf_op jit(solution)/shard_map/all_to_all | solution.py:190
  26.2 141.3 %all-gather.2.cloned.1.call-start = ((), (), s32[]{:S(2)}) async-start(), calls=%async_computation.5 | async-start | bytes 7864320 | tf_op jit(solution)/shard_map/all_gather | solution.py:204
  27.2 41.1 %collective-permute-start = (bf16[64,32,128]{2,1,0:T(8,128)(2,1)}, bf16[64,32,128]{2,1,0:T(8,128)(2,1)}, u32[]{:S(2)}, u32[]{:S(2)}) collective-permute-start(bf16[64,32,128]{2,1,0:T(8,128)(2,1)} %slice.79), channel_id=1, source_target_pairs={{0,1},{1,2},{2,3},{3,0},{4,5},{5,6},{6,7},{7,4},{8,9},{9,10},{10,1... | collective-permute-start | bytes 1572872 | tf_op jit(solution)/shard_map/ppermute | solution.py:25
  28.4 39.9 %collective-permute-start.1 = (bf16[64,32,128]{2,1,0:T(8,128)(2,1)}, bf16[64,32,128]{2,1,0:T(8,128)(2,1)}, u32[]{:S(2)}, u32[]{:S(2)}) collective-permute-start(bf16[64,32,128]{2,1,0:T(8,128)(2,1)} %slice.79), channel_id=1, source_target_pairs={{0,3},{1,0},{2,1},{3,2},{4,7},{5,4},{6,5},{7,6},{8,11},{9,8},{10,9... | collective-permute-start | bytes 1572872 | tf_op jit(solution)/shard_map/ppermute | solution.py:25
  29.8 38.4 %collective-permute-start.2 = (bf16[64,32,128]{2,1,0:T(8,128)(2,1)}, bf16[64,32,128]{2,1,0:T(8,128)(2,1)}, u32[]{:S(2)}, u32[]{:S(2)}) collective-permute-start(bf16[64,32,128]{2,1,0:T(8,128)(2,1)} %slice.79), channel_id=1, source_target_pairs={{0,2},{1,3},{2,0},{3,1},{4,6},{5,7},{6,4},{7,5},{8,10},{9,11},{10,... | collective-permute-start | bytes 1572872 | tf_op jit(solution)/shard_map/ppermute | solution.py:25
  69.4 34.7 %all-to-all-start.1 = ((bf16[64,64,128]{2,1,0:T(8,128)(2,1)}), bf16[64,64,128]{2,1,0:T(8,128)(2,1)S(1)}, u32[]{:S(2)}, u32[]{:S(2)}) async-start(bf16[64,64,128]{2,1,0:T(8,128)(2,1)} %slice.80), calls=%async_computation.1 | async-start | bytes 2097152 | tf_op jit(solution)/shard_map/all_to_all | solution.py:190
  104.1 79.8 %all-to-all-start.2 = ((bf16[64,128,128]{2,1,0:T(8,128)(2,1)}), bf16[64,128,128]{2,1,0:T(8,128)(2,1)S(1)}, u32[]{:S(2)}, u32[]{:S(2)}) async-start(bf16[64,128,128]{2,1,0:T(8,128)(2,1)} %pad_maximum_fusion), calls=%async_computation.2 | async-start | bytes 4194304 | tf_op jit(solution)/shard_map/all_to_all | solution.py:190
  110.6 57.0 %copy-start.2 = (bf16[8,8,32,128]{3,1,2,0:T(8,128)(2,1)}, bf16[8,8,32,128]{3,1,2,0:T(8,128)(2,1)S(1)}, u32[]{:S(2)}) copy-start(bf16[8,8,32,128]{3,1,2,0:T(8,128)(2,1)S(1)} %copy.39) | copy-start | bytes 1572868
  110.8 56.7 %copy-start.3 = (bf16[8,8,32,128]{3,1,2,0:T(8,128)(2,1)}, bf16[8,8,32,128]{3,1,2,0:T(8,128)(2,1)S(1)}, u32[]{:S(2)}) copy-start(bf16[8,8,32,128]{3,1,2,0:T(8,128)(2,1)S(1)} %copy.38) | copy-start | bytes 1572868
  110.8 26.2 %collective-permute-start.3 = (bf16[64,4096]{1,0:T(8,128)(2,1)S(1)}, bf16[64,4096]{1,0:T(8,128)(2,1)S(1)}, u32[]{:S(2)}, u32[]{:S(2)}) collective-permute-start(bf16[64,4096]{1,0:T(8,128)(2,1)S(1)} %bitcast.64), channel_id=1, source_target_pairs={{0,1},{1,2},{2,3},{3,0},{4,5},{5,6},{6,7},{7,4},{8,9},{9,10},{10,1... | collective-permute-start | bytes 1572872 | tf_op jit(solution)/shard_map/ppermute | solution.py:25
  112.1 25.0 %collective-permute-start.6 = (bf16[64,4096]{1,0:T(8,128)(2,1)S(1)}, bf16[64,4096]{1,0:T(8,128)(2,1)S(1)}, u32[]{:S(2)}, u32[]{:S(2)}) collective-permute-start(bf16[64,4096]{1,0:T(8,128)(2,1)S(1)} %bitcast.68), channel_id=1, source_target_pairs={{0,3},{1,0},{2,1},{3,2},{4,7},{5,4},{6,5},{7,6},{8,11},{9,8},{10,9... | collective-permute-start | bytes 1572872 | tf_op jit(solution)/shard_map/ppermute | solution.py:25
  113.6 41.9 %collective-permute-start.4 = (bf16[64,4096]{1,0:T(8,128)(2,1)S(1)}, bf16[64,4096]{1,0:T(8,128)(2,1)S(1)}, u32[]{:S(2)}, u32[]{:S(2)}) collective-permute-start(bf16[64,4096]{1,0:T(8,128)(2,1)S(1)} %bitcast.69), channel_id=1, source_target_pairs={{0,1},{1,2},{2,3},{3,0},{4,5},{5,6},{6,7},{7,4},{8,9},{9,10},{10,1... | collective-permute-start | bytes 1572872 | tf_op jit(solution)/shard_map/ppermute | solution.py:25
  113.6 41.9 %collective-permute-start.5 = (bf16[64,4096]{1,0:T(8,128)(2,1)S(1)}, bf16[64,4096]{1,0:T(8,128)(2,1)S(1)}, u32[]{:S(2)}, u32[]{:S(2)}) collective-permute-start(bf16[64,4096]{1,0:T(8,128)(2,1)S(1)} %bitcast.65), channel_id=1, source_target_pairs={{0,3},{1,0},{2,1},{3,2},{4,7},{5,4},{6,5},{7,6},{8,11},{9,8},{10,9... | collective-permute-start | bytes 1572872 | tf_op jit(solution)/shard_map/ppermute | solution.py:25
  137.1 18.4 %copy-start.4 = (bf16[64,4096]{1,0:T(8,128)(2,1)}, bf16[64,4096]{1,0:T(8,128)(2,1)S(1)}, u32[]{:S(2)}) copy-start(bf16[64,4096]{1,0:T(8,128)(2,1)S(1)} %collective-permute-done.3.refs_4_) | copy-start | bytes 1572868
  137.1 29.6 %collective-permute-start.7 = (bf16[64,4096]{1,0:T(8,128)(2,1)S(1)}, bf16[64,4096]{1,0:T(8,128)(2,1)S(1)}, u32[]{:S(2)}, u32[]{:S(2)}) collective-permute-start(bf16[64,4096]{1,0:T(8,128)(2,1)S(1)} %collective-permute-done.3.refs_4_), channel_id=1, source_target_pairs={{0,1},{1,2},{2,3},{3,0},{4,5},{5,6},{6,7},{7,4},{8,9},{9,10},{10,1... | collective-permute-start | bytes 1572872 | tf_op jit(solution)/shard_map/ppermute | solution.py:25
  137.1 29.6 %copy-start.5 = (bf16[64,4096]{1,0:T(8,128)(2,1)}, bf16[64,4096]{1,0:T(8,128)(2,1)S(1)}, u32[]{:S(2)}) copy-start(bf16[64,4096]{1,0:T(8,128)(2,1)S(1)} %collective-permute-done.6.refs_7_) | copy-start | bytes 1572868
  137.1 30.5 %collective-permute-start.8 = (bf16[64,4096]{1,0:T(8,128)(2,1)S(1)}, bf16[64,4096]{1,0:T(8,128)(2,1)}, u32[]{:S(2)}, u32[]{:S(2)}) collective-permute-start(bf16[64,4096]{1,0:T(8,128)(2,1)S(1)} %collective-permute-done.6.refs_7_), channel_id=1, source_target_pairs={{0,3},{1,0},{2,1},{3,2},{4,7},{5,4},{6,5},{7,6},{8,11},{9,8},{10,9... | collective-permute-start | bytes 1572872 | tf_op jit(solution)/shard_map/ppermute | solution.py:25
  155.5 11.2 %copy-start.6 = (bf16[64,4096]{1,0:T(8,128)(2,1)}, bf16[64,4096]{1,0:T(8,128)(2,1)S(1)}, u32[]{:S(2)}) copy-start(bf16[64,4096]{1,0:T(8,128)(2,1)S(1)} %collective-permute-done.4.refs_5_) | copy-start | bytes 1572868
  155.5 11.2 %copy-start.7 = (bf16[64,4096]{1,0:T(8,128)(2,1)}, bf16[64,4096]{1,0:T(8,128)(2,1)S(1)}, u32[]{:S(2)}) copy-start(bf16[64,4096]{1,0:T(8,128)(2,1)S(1)} %collective-permute-done.5.refs_6_) | copy-start | bytes 1572868
  166.7 0.8 copy-start.8
  181.1 26.5 %collective-permute-start.12 = (bf16[128,4224]{1,0:T(8,128)(2,1)}, bf16[128,4224]{1,0:T(8,128)(2,1)S(1)}, u32[]{:S(2)}, u32[]{:S(2)}) collective-permute-start(bf16[128,4224]{1,0:T(8,128)(2,1)} %get-tuple-element.38), channel_id=1, source_target_pairs={{0,2},{1,3},{2,0},{3,1},{4,6},{5,7},{6,4},{7,5},{8,10},{9,11},{10,... | collective-permute-start | bytes 3244040 | tf_op jit(solution)/shard_map/ppermute | solution.py:25
  182.4 46.9 %collective-permute-start.13 = (bf16[128,4224]{1,0:T(8,128)(2,1)}, bf16[128,4224]{1,0:T(8,128)(2,1)}, u32[]{:S(2)}, u32[]{:S(2)}) collective-permute-start(bf16[128,4224]{1,0:T(8,128)(2,1)} %get-tuple-element.39), channel_id=1, source_target_pairs={{0,3},{1,0},{2,1},{3,2},{4,7},{5,4},{6,5},{7,6},{8,11},{9,8},{10,9... | collective-permute-start | bytes 3244040 | tf_op jit(solution)/shard_map/ppermute | solution.py:25
  183.6 48.3 %collective-permute-start.14 = (bf16[128,4224]{1,0:T(8,128)(2,1)}, bf16[128,4224]{1,0:T(8,128)(2,1)}, u32[]{:S(2)}, u32[]{:S(2)}) collective-permute-start(bf16[128,4224]{1,0:T(8,128)(2,1)} %get-tuple-element.40), channel_id=1, source_target_pairs={{0,1},{1,2},{2,3},{3,0},{4,5},{5,6},{6,7},{7,4},{8,9},{9,10},{10,1... | collective-permute-start | bytes 3244040 | tf_op jit(solution)/shard_map/ppermute | solution.py:25
  188.4 43.6 %copy-start.9 = (bf16[128,4224]{1,0:T(8,128)(2,1)S(1)}, bf16[128,4224]{1,0:T(8,128)(2,1)}, u32[]{:S(2)}) copy-start(bf16[128,4224]{1,0:T(8,128)(2,1)} %get-tuple-element.42) | copy-start | bytes 3244036
  197.6 48.5 %collective-permute-start.11 = (bf16[64,4224]{1,0:T(8,128)(2,1)}, bf16[64,4224]{1,0:T(8,128)(2,1)}, u32[]{:S(2)}, u32[]{:S(2)}) collective-permute-start(bf16[64,4224]{1,0:T(8,128)(2,1)} %get-tuple-element.36), channel_id=1, source_target_pairs={{0,1},{1,2},{2,3},{3,0},{4,5},{5,6},{6,7},{7,4},{8,9},{9,10},{10,1... | collective-permute-start | bytes 1622024 | tf_op jit(solution)/shard_map/ppermute | solution.py:25
  197.7 48.4 %collective-permute-start.10 = (bf16[64,4224]{1,0:T(8,128)(2,1)}, bf16[64,4224]{1,0:T(8,128)(2,1)}, u32[]{:S(2)}, u32[]{:S(2)}) collective-permute-start(bf16[64,4224]{1,0:T(8,128)(2,1)} %get-tuple-element.35), channel_id=1, source_target_pairs={{0,3},{1,0},{2,1},{3,2},{4,7},{5,4},{6,5},{7,6},{8,11},{9,8},{10,9... | collective-permute-start | bytes 1622024 | tf_op jit(solution)/shard_map/ppermute | solution.py:25
  207.6 46.5 %collective-permute-start.9 = (bf16[64,4224]{1,0:T(8,128)(2,1)}, bf16[64,4224]{1,0:T(8,128)(2,1)}, u32[]{:S(2)}, u32[]{:S(2)}) collective-permute-start(bf16[64,4224]{1,0:T(8,128)(2,1)} %get-tuple-element.34), channel_id=1, source_target_pairs={{0,2},{1,3},{2,0},{3,1},{4,6},{5,7},{6,4},{7,5},{8,10},{9,11},{10,... | collective-permute-start | bytes 1622024 | tf_op jit(solution)/shard_map/ppermute | solution.py:25
  234.2 19.9 %copy-start.11 = (bf16[64,4224]{1,0:T(8,128)(2,1)S(1)}, bf16[64,4224]{1,0:T(8,128)(2,1)}, u32[]{:S(2)}) copy-start(bf16[64,4224]{1,0:T(8,128)(2,1)} %get-tuple-element.33) | copy-start | bytes 1622020
  235.5 39.2 %all-to-all-start.3 = ((bf16[64,64,128]{2,1,0:T(8,128)(2,1)}), bf16[64,64,128]{2,1,0:T(8,128)(2,1)S(1)}, u32[]{:S(2)}, u32[]{:S(2)}) async-start(bf16[64,64,128]{2,1,0:T(8,128)(2,1)} %bitcast.27), calls=%async_computation.3 | async-start | bytes 2097152 | tf_op jit(solution)/shard_map/all_to_all | solution.py:190
  275.8 26.4 %all-to-all-start.4 = ((bf16[64,35,128]{2,1,0:T(8,128)(2,1)}), bf16[64,35,128]{2,1,0:T(8,128)(2,1)}, u32[]{:S(2)}, u32[]{:S(2)}) async-start(bf16[64,35,128]{2,1,0:T(8,128)(2,1)} %reshape.84), calls=%async_computation.4 | async-start | bytes 1310720 | tf_op jit(solution)/shard_map/all_to_all | solution.py:190
  302.2 4.0 %copy-start.1 = (bf16[128,4096]{1,0:T(8,128)(2,1)S(1)}, bf16[128,4096]{1,0:T(8,128)(2,1)}, u32[]{:S(2)}) copy-start(bf16[128,4096]{1,0:T(8,128)(2,1)} %param.6) | copy-start | bytes 3145732
Sparse Core Ops, SparseCore 0:
  68.4 82.9 all-gather.1
where the time goes:
time: 314 us; the launch traced here: 313 us
  waiting for transfers between devices  174 us (55%)
  starting transfers between devices  61.6 us (20%)
  Pallas kernels  31.5 us (10%)
  local copies, waits for them, and re-layouts  16.8 us (5%)
  between operations  14.4 us (5%)
  other arithmetic  9.83 us (3%)
  matrix products  4.51 us (1%)
    all_to_all x5, waiting for transfers between devices, exchange(): lax.all_to_all(value, 'expert', split_axis=0, concat_axis=0, tiled=True)  88.4 us
    ppermute x15, waiting for transfers between devices, shift(): lax.ppermute(value, 'tensor', [(i, (i + step) % size) for i in range(size)])  86.1 us
    all_to_all x5, starting transfers between devices, exchange(): lax.all_to_all(value, 'expert', split_axis=0, concat_axis=0, tiled=True)  42.5 us
    pallas_call x2, Pallas kernels, expert_math(): pl.pallas_call(functools.partial(expert_kernel, begin, count), out_shape=...  22.8 us
    ppermute x15, starting transfers between devices, shift(): lax.ppermute(value, 'tensor', [(i, (i + step) % size) for i in range(size)])  19.1 us
    unnamed x36, local copies, waits for them, and re-layouts  8.73 us
    pallas_call x1, Pallas kernels, weight_grad(): pl.pallas_call(functools.partial(weight_grad_kernel, counts), grid=(8,),...  8.69 us
  transfers between devices with their start and end apart: 21, of which 11 were waited for; matrix products, arithmetic and copies ran while one was open for 6% of the time, Pallas kernels for 10%

commit v1 on v0

--- a/solution.py
+++ b/solution.py
@@ -54,8 +54,9 @@
 def expert_kernel(begin, count, *refs):
     place, tokens, grads = refs[0], refs[1], refs[2 : 2 + count]
     w_in, w_out, activated_ref = refs[2 + count : 5 + count]
-    partials = refs[5 + count : 9 + count]
-    rows, grad_rows, w_in_v, w_out_v, result, sems, grad_sems, out_sems = refs[9 + count :]
+    split = count // 4
+    partials = refs[5 + count : 5 + 2 * count]
+    rows, grad_rows, w_in_v, w_out_v, result, sems, grad_sems, out_sems = refs[5 + 2 * count :]
     piece, width = grads[0].shape
     n = piece * count // 4
     block = tokens.shape[0] // 4
@@ -86,8 +87,8 @@
         rows_of = slice(pair * 2 * n, (pair + 1) * 2 * n)
         part = lax.dot_general(grad_pre[rows_of], w_in_v[...], TRANSPOSED, preferred_element_type=jnp.float32)
         result[rows_of, :width] = part.astype(jnp.bfloat16)
-        for i in (2 * pair, 2 * pair + 1):
-            stores.append(pltpu.make_async_copy(result.at[pl.ds(i * n, n)], partials[i], out_sems.at[i]))
+        for i in range(2 * pair * split, 2 * (pair + 1) * split):
+            stores.append(pltpu.make_async_copy(result.at[pl.ds(i * piece, piece)], partials[i], out_sems.at[i]))
             stores[-1].start()
     wait_all(stores)
 
@@ -100,9 +101,9 @@
     outs = pl.pallas_call(
         functools.partial(expert_kernel, begin, count),
         out_shape=[jax.ShapeDtypeStruct((4 * n, hidden), bf16)]
-        + [jax.ShapeDtypeStruct((n, width + 128), bf16)] * 4,
+        + [jax.ShapeDtypeStruct((piece, width + 128), bf16)] * count,
         in_specs=[pl.BlockSpec(memory_space=pltpu.SMEM)] + [HBM] * (3 + count),
-        out_specs=[pl.BlockSpec(memory_space=pltpu.VMEM)] + [HBM] * 4,
+        out_specs=[pl.BlockSpec(memory_space=pltpu.VMEM)] + [HBM] * count,
         scratch_shapes=[
             pltpu.VMEM((4 * n, width), bf16),
             pltpu.VMEM((4 * n, width), bf16),
@@ -111,7 +112,7 @@
             pltpu.VMEM((4 * n, width + 128), bf16),
             pltpu.SemaphoreType.DMA((6,)),
             pltpu.SemaphoreType.DMA((8,)),
-            pltpu.SemaphoreType.DMA((4,)),
+            pltpu.SemaphoreType.DMA((8,)),
         ],
         compiler_params=PARAMS,
         name="expert",
@@ -207,21 +208,28 @@
     ring, _ = ring_gather(by_slot(there, 0), by_slot(there, 1))
     grads = [ring]
     place = lax.axis_index("tensor").reshape(1)
-    acts, parts, sums = [], [], []
-    for turn in range(2):
-        begin = turn * (CAP - 1) * experts
-        if turn == 1:
-            grads.append(tuple(by_slot(after(whole, acts[0]), i) for i in range(4)))
-        activated, (own, left, right, far) = expert_math(begin, place, tokens, grads[turn], w_in, w_out)
-        acts.append(activated)
-        parts.append([own, shift(far, 2), shift(left, -1), shift(right, 1)])
-    parts[0] = after(parts[0], acts[1])
-    for turn in range(2):
-        if turn == 1:
-            pair = jnp.concatenate([sums[0][:experts, :width], sums[0][experts:, :width]], axis=1)
-            back = exchange(pair.reshape(experts, 2 * blocks, 128))
-        sums.append(sum(part.astype(jnp.float32) for part in parts[turn]).astype(jnp.bfloat16))
-    slotwise = [sums[0][:experts], sums[0][experts:], sums[1]]
+    f32, bf16 = jnp.float32, jnp.bfloat16
+
+    def total(*values):
+        return sum(value.astype(f32) for value in values).astype(bf16)
+
+    first, ends = expert_math(0, place, tokens, grads[0], w_in, w_out)
+    own, left, right, far = ends[0:2], ends[2:4], ends[4:6], ends[6:8]
+    from_left, from_right = shift(far[1], 1), shift(far[0], -1)
+    plain_right, plain_left = shift(right[0], 1), shift(left[1], -1)
+    pieces = tuple(by_slot(after(whole, first), i) for i in range(4))
+    grads.append(pieces)
+    second, ends = expert_math((CAP - 1) * experts, place, tokens, pieces, w_in, w_out)
+    acts = [first, second]
+    from_left, from_right = after((from_left, from_right), second)
+    both_right = shift(total(right[1], from_left), 1)
+    both_left = shift(total(left[0], from_right), -1)
+    lone = [ends[0], shift(ends[3], 2), shift(ends[1], -1), shift(ends[2], 1)]
+    upper, lower = total(own[0], plain_right, both_left), total(own[1], both_right, plain_left)
+    pair = jnp.concatenate([upper[:, :width], lower[:, :width]], axis=1)
+    back = exchange(pair.reshape(experts, 2 * blocks, 128))
+    sums = [None, total(*lone)]
+    slotwise = [upper, lower, sums[1]]
     rest = [sums[1][:, :width]] + [part[:, width:] for part in slotwise]
     rest, acts[0], back = lax.optimization_barrier((jnp.concatenate(rest, axis=1), acts[0], back))
     rest = exchange(rest.reshape(experts, -1, 128)).reshape(experts, -1)

time: 314 us -> 330 us (1.051)
  waiting for transfers between devices: 174 us -> 186 us
  starting transfers between devices: 61.6 us -> 67.1 us
    all_to_all x5, waiting for transfers between devices: 88.4 us -> 96.3 us  [exchange(): lax.all_to_all(value, 'expert', split_axis=0, concat_axis=0, tiled=True)]
    ppermute x15 -> x18, waiting for transfers between devices: 86.1 us -> 90.1 us  [shift(): lax.ppermute(value, 'tensor', [(i, (i + step) % size) for i in range(size)])]
    ppermute x15 -> x18, starting transfers between devices: 19.1 us -> 21.9 us  [shift(): lax.ppermute(value, 'tensor', [(i, (i + step) % size) for i in range(size)])]
    unnamed x36 -> x46, local copies, waits for them, and re-layouts: 8.73 us -> 8.7 us
  transfers between devices with their start and end apart: 21 -> 24, of which waited for: 11 -> 10; matrix products, arithmetic and copies ran while one was open for 6% -> 5% of each run, Pallas kernels for 10% -> 10%
where the time goes in v1:
time: 330 us; the launch traced here: 329 us
  waiting for transfers between devices  186 us (56%)
  starting transfers between devices  67.1 us (20%)
  Pallas kernels  31.5 us (10%)
  local copies, waits for them, and re-layouts  16.7 us (5%)
  between operations  14.5 us (4%)
  other arithmetic  8.4 us (3%)
  matrix products  4.5 us (1%)
    all_to_all x5, waiting for transfers between devices, exchange(): lax.all_to_all(value, 'expert', split_axis=0, concat_axis=0, tiled=True)  96.3 us
    ppermute x18, waiting for transfers between devices, shift(): lax.ppermute(value, 'tensor', [(i, (i + step) % size) for i in range(size)])  90.1 us
    all_to_all x5, starting transfers between devices, exchange(): lax.all_to_all(value, 'expert', split_axis=0, concat_axis=0, tiled=True)  45.2 us
    pallas_call x2, Pallas kernels, expert_math(): pl.pallas_call(functools.partial(expert_kernel, begin, count), out_shape=...  22.8 us
    ppermute x18, starting transfers between devices, shift(): lax.ppermute(value, 'tensor', [(i, (i + step) % size) for i in range(size)])  21.9 us
    unnamed x46, local copies, waits for them, and re-layouts  8.7 us
    pallas_call x1, Pallas kernels, weight_grad(): pl.pallas_call(functools.partial(weight_grad_kernel, counts), grid=(8,),...  8.69 us
  transfers between devices with their start and end apart: 24, of which 10 were waited for; matrix products, arithmetic and copies ran while one was open for 5% of the time, Pallas kernels for 10%

profile of v1, /device:TPU:1, one launch (start us, length us, event | category | flops | bytes accessed | tf_op | source)
XLA Modules:
  0.0 329.2 jit_solution(5067020234548037462)
XLA Ops:
  7.2 0.7 fusion.35
  8.1 0.7 fusion.34
  8.8 0.7 convolution_convert_fusion.1
  9.5 2.1 reshape.71
  11.6 0.7 convolution_convert_fusion
  12.3 0.8 reshape.72
  13.1 13.2 %all-to-all-start = ((bf16[64,96,128]{2,1,0:T(8,128)(2,1)}), bf16[64,96,128]{2,1,0:T(8,128)(2,1)S(1)}, u32[]{:S(2)}, u32[]{:S(2)}) async-start(bf16[64,96,128]{2,1,0:T(8,128)(2,1)} %reshape.71), calls=%async_computation | async-start | bytes 3145728 | tf_op jit(solution)/shard_map/all_to_all | solution.py:191
  26.3 0.9 slice.75
  27.2 1.2 collective-permute-start
  28.4 1.5 collective-permute-start.1
  29.9 1.5 collective-permute-start.2
  31.4 34.6 %all-to-all-done = bf16[64,96,128]{2,1,0:T(8,128)(2,1)S(1)} async-done(((bf16[64,96,128]{2,1,0:T(8,128)(2,1)}), bf16[64,96,128]{2,1,0:T(8,128)(2,1)S(1)}, u32[]{:S(2)}, u32[]{:S(2)}) %all-to-all-start) | async-done | bytes 1572896 | tf_op jit(solution)/shard_map/all_to_all | solution.py:191
  66.0 0.3 fusion.37
  66.3 0.4 copy_bitcast_fusion.8
  66.7 0.2 copy.40
  66.9 1.3 pad_maximum_fusion.1
  68.3 1.1 slice.76
  69.4 6.1 %all-to-all-start.1 = ((bf16[64,64,128]{2,1,0:T(8,128)(2,1)}), bf16[64,64,128]{2,1,0:T(8,128)(2,1)S(1)}, u32[]{:S(2)}, u32[]{:S(2)}) async-start(bf16[64,64,128]{2,1,0:T(8,128)(2,1)} %slice.76), calls=%async_computation.1 | async-start | bytes 2097152 | tf_op jit(solution)/shard_map/all_to_all | solution.py:191
  75.5 3.3 %pad_maximum_fusion = bf16[64,128,128]{2,1,0:T(8,128)(2,1)} fusion(bf16[64,32,128]{2,1,0:T(8,128)(2,1)} %collective-permute-done.2, bf16[64,32,128]{2,1,0:T(8,128)(2,1)} %collective-permute-done.1, bf16[64,32,128]{2,1,0:T(8,128)(2,1)} %collective-permute-done, bf16[64,32,128]{2,1,0:T(8,128)(2,1)} %slice.75), kind=kLoop, calls=%fused_computation.5 | loop fusion | flops 8388608 | bytes 4194304 | tf_op jit(solution)/shard_map/concatenate | solution.py:207
  78.9 25.2 %all-to-all-done.1 = bf16[64,64,128]{2,1,0:T(8,128)(2,1)S(1)} async-done(((bf16[64,64,128]{2,1,0:T(8,128)(2,1)}), bf16[64,64,128]{2,1,0:T(8,128)(2,1)S(1)}, u32[]{:S(2)}, u32[]{:S(2)}) %all-to-all-start.1) | async-done | bytes 1048608 | tf_op jit(solution)/shard_map/all_to_all | solution.py:191
  104.1 6.2 %all-to-all-start.2 = ((bf16[64,128,128]{2,1,0:T(8,128)(2,1)}), bf16[64,128,128]{2,1,0:T(8,128)(2,1)S(1)}, u32[]{:S(2)}, u32[]{:S(2)}) async-start(bf16[64,128,128]{2,1,0:T(8,128)(2,1)} %pad_maximum_fusion), calls=%async_computation.2 | async-start | bytes 4194304 | tf_op jit(solution)/shard_map/all_to_all | solution.py:191
  110.4 0.2 copy.39
  110.6 0.2 copy.38
  110.8 1.3 collective-permute-start.3
  112.1 1.5 collective-permute-start.6
  113.6 2.7 collective-permute-start.5
  116.3 20.8 %collective-permute-done.3.refs_4_ = bf16[64,4096]{1,0:T(8,128)(2,1)S(1)} collective-permute-done((bf16[64,4096]{1,0:T(8,128)(2,1)S(1)}, bf16[64,4096]{1,0:T(8,128)(2,1)S(1)}, u32[]{:S(2)}, u32[]{:S(2)}) %collective-permute-start.3) | collective-permute-done | bytes 524320 | tf_op jit(solution)/shard_map/ppermute | solution.py:25
  137.1 2.7 collective-permute-start.8
  139.7 15.7 %collective-permute-done.4.refs_5_ = bf16[64,4096]{1,0:T(8,128)(2,1)S(1)} collective-permute-done((bf16[64,4096]{1,0:T(8,128)(2,1)S(1)}, bf16[64,4096]{1,0:T(8,128)(2,1)S(1)}, u32[]{:S(2)}, u32[]{:S(2)}) %collective-permute-start.4) | collective-permute-done | bytes 524320 | tf_op jit(solution)/shard_map/ppermute | solution.py:25
  155.5 11.2 %collective-permute-done.7.refs_8_ = bf16[64,4096]{1,0:T(8,128)(2,1)S(1)} collective-permute-done((bf16[64,4096]{1,0:T(8,128)(2,1)S(1)}, bf16[64,4096]{1,0:T(8,128)(2,1)S(1)}, u32[]{:S(2)}, u32[]{:S(2)}) %collective-permute-start.7) | collective-permute-done | bytes 524320 | tf_op jit(solution)/shard_map/ppermute | solution.py:25
  166.7 0.8 copy-done.8
  167.5 13.5 %expert.2 = (bf16[512,384]{1,0:T(8,128)(2,1)}, bf16[64,4224]{1,0:T(8,128)(2,1)}, bf16[64,4224]{1,0:T(8,128)(2,1)}, bf16[64,4224]{1,0:T(8,128)(2,1)}, bf16[64,422...) custom-call(s32[1]{0:T(128)} %bitcast.3.refs_0_, ...), custom_call_target="tpu_custom_call" | custom-call | tf_op jit(solution)/shard_map/expert/pallas_call | solution.py:101
  181.2 2.6 collective-permute-start.14
  183.8 0.4 fusion.36
  184.2 1.0 copy.37
  185.2 1.0 copy.36
  186.3 1.0 copy.35
  187.3 1.0 copy.34
  188.3 9.3 %expert.3 = (bf16[256,384]{1,0:T(8,128)(2,1)}, bf16[64,4224]{1,0:T(8,128)(2,1)}, bf16[64,4224]{1,0:T(8,128)(2,1)}, bf16[64,4224]{1,0:T(8,128)(2,1)}, bf16[64,4224]{1,0:T(8,128)(2,1)}) custom-call(s32[1]{0:T(128)} %bitcast.3.refs_0_, bf16[768,4096]{1,0:T(8,128)(2,1)} %all-gather.2.cloned.1.call-done.refs_1_, bf16[64,4096]{1,0:T(8,128)(2,1)} %bitcast.72, ...), custom_call_target="tpu_custom_call" | custom-call | tf_op jit(solution)/shard_map/expert/pallas_call | solution.py:101
  197.7 2.7 collective-permute-start.10
  200.4 1.3 collective-permute-start.17
  201.8 0.4 collective-permute-start.16
  202.3 31.5 %collective-permute-done.17 = bf16[64,4224]{1,0:T(8,128)(2,1)S(1)} collective-permute-done((bf16[64,4224]{1,0:T(8,128)(2,1)S(1)}, bf16[64,4224]{1,0:T(8,128)(2,1)S(1)}, u32[]{:S(2)}, u32[]{:S(2)}) %collective-permute-start.17) | collective-permute-done | bytes 540704 | tf_op jit(solution)/shard_map/ppermute | solution.py:25
  233.8 1.0 collective-permute-done.16
  234.8 2.5 collective-permute-start.15
  237.3 0.2 add_convert_fusion
  237.5 9.8 %collective-permute-done.12 = bf16[64,4224]{1,0:T(8,128)(2,1)S(1)} collective-permute-done((bf16[64,4224]{1,0:T(8,128)(2,1)S(1)}, bf16[64,4224]{1,0:T(8,128)(2,1)S(1)}, u32[]{:S(2)}, u32[]{:S(2)}) %collective-permute-start.12) | collective-permute-done | bytes 540704 | tf_op jit(solution)/shard_map/ppermute | solution.py:25
  247.7 1.3 copy.18
  249.0 13.3 %all-to-all-start.3 = ((bf16[64,64,128]{2,1,0:T(8,128)(2,1)}), bf16[64,64,128]{2,1,0:T(8,128)(2,1)S(1)}, u32[]{:S(2)}, u32[]{:S(2)}) async-start(bf16[64,64,128]{2,1,0:T(8,128)(2,1)} %bitcast.27), calls=%async_computation.3 | async-start | bytes 2097152 | tf_op jit(solution)/shard_map/all_to_all | solution.py:191
  262.4 1.6 add_convert_fusion.4
  264.1 26.7 %all-to-all-done.3 = bf16[64,64,128]{2,1,0:T(8,128)(2,1)S(1)} async-done(((bf16[64,64,128]{2,1,0:T(8,128)(2,1)}), bf16[64,64,128]{2,1,0:T(8,128)(2,1)S(1)}, u32[]{:S(2)}, u32[]{:S(2)}) %all-to-all-start.3) | async-done | bytes 1048608 | tf_op jit(solution)/shard_map/all_to_all | solution.py:191
  290.9 1.1 reshape.84
  292.0 6.4 %all-to-all-start.4 = ((bf16[64,35,128]{2,1,0:T(8,128)(2,1)}), bf16[64,35,128]{2,1,0:T(8,128)(2,1)}, u32[]{:S(2)}, u32[]{:S(2)}) async-start(bf16[64,35,128]{2,1,0:T(8,128)(2,1)} %reshape.84), calls=%async_computation.4 | async-start | bytes 1310720 | tf_op jit(solution)/shard_map/all_to_all | solution.py:191
  298.4 0.7 copy.32
  299.1 8.7 %weight_grad.1 = bf16[384,4096]{1,0:T(8,128)(2,1)} custom-call(bf16[512,384]{1,0:T(8,128)(2,1)} %get-tuple-element.52.refs_0_, bf16[256,384]{1,0:T(8,128)(2,1)} %get-tuple-element.44.refs_1_, bf16[64,4096]{1,0:T(8,128)(2,1)} %bitcast.67, bf16[64,4096]{1,0:T(8,128)(2,1)} %bitcast.71, bf16[64,4096]{1,0:T(8,128)(2,1)} %copy-done.4, bf16[64,4096]{1,0:T(8,128)(2,1)} %copy-done.6, ...), custom_call_target="tpu_custom_call" | custom-call | tf_op jit(solution)/shard_map/weight_grad/pallas_call | solution.py:161
  307.8 0.5 fusion.4
  308.3 0.5 convolution_add_fusion.1
  308.8 9.7 %all-to-all-done.4 = bf16[64,35,128]{2,1,0:T(8,128)(2,1)} async-done(((bf16[64,35,128]{2,1,0:T(8,128)(2,1)}), bf16[64,35,128]{2,1,0:T(8,128)(2,1)}, u32[]{:S(2)}, u32[]{:S(2)}) %all-to-all-start.4) | async-done | bytes 573472 | tf_op jit(solution)/shard_map/all_to_all | solution.py:191
  318.4 1.2 copy.33
  319.6 0.2 fusion.9
  319.8 0.2 fusion.12
  320.1 0.2 fusion.6
  320.3 1.5 fusion
  321.8 0.5 fusion.33
  (74 shorter events, 1.4 us)
Async XLA Ops:
  7.2 1.6 copy-start
  9.5 2.1 copy-start.15
  9.5 2.1 copy-start.9
  13.1 53.0 %all-to-all-start = ((bf16[64,96,128]{2,1,0:T(8,128)(2,1)}), bf16[64,96,128]{2,1,0:T(8,128)(2,1)S(1)}, u32[]{:S(2)}, u32[]{:S(2)}) async-start(bf16[64,96,128]{2,1,0:T(8,128)(2,1)} %reshape.71), calls=%async_computation | async-start | bytes 3145728 | tf_op jit(solution)/shard_map/all_to_all | solution.py:191
  26.2 141.3 %all-gather.2.cloned.1.call-start = ((), (), s32[]{:S(2)}) async-start(), calls=%async_computation.5 | async-start | bytes 7864320 | tf_op jit(solution)/shard_map/all_gather | solution.py:205
  27.2 41.1 %collective-permute-start = (bf16[64,32,128]{2,1,0:T(8,128)(2,1)}, bf16[64,32,128]{2,1,0:T(8,128)(2,1)}, u32[]{:S(2)}, u32[]{:S(2)}) collective-permute-start(bf16[64,32,128]{2,1,0:T(8,128)(2,1)} %slice.75), channel_id=1, source_target_pairs={{0,1},{1,2},{2,3},{3,0},{4,5},{5,6},{6,7},{7,4},{8,9},{9,10},{10,1... | collective-permute-start | bytes 1572872 | tf_op jit(solution)/shard_map/ppermute | solution.py:25
  28.4 39.8 %collective-permute-start.1 = (bf16[64,32,128]{2,1,0:T(8,128)(2,1)}, bf16[64,32,128]{2,1,0:T(8,128)(2,1)}, u32[]{:S(2)}, u32[]{:S(2)}) collective-permute-start(bf16[64,32,128]{2,1,0:T(8,128)(2,1)} %slice.75), channel_id=1, source_target_pairs={{0,3},{1,0},{2,1},{3,2},{4,7},{5,4},{6,5},{7,6},{8,11},{9,8},{10,9... | collective-permute-start | bytes 1572872 | tf_op jit(solution)/shard_map/ppermute | solution.py:25
  29.9 38.4 %collective-permute-start.2 = (bf16[64,32,128]{2,1,0:T(8,128)(2,1)}, bf16[64,32,128]{2,1,0:T(8,128)(2,1)}, u32[]{:S(2)}, u32[]{:S(2)}) collective-permute-start(bf16[64,32,128]{2,1,0:T(8,128)(2,1)} %slice.75), channel_id=1, source_target_pairs={{0,2},{1,3},{2,0},{3,1},{4,6},{5,7},{6,4},{7,5},{8,10},{9,11},{10,... | collective-permute-start | bytes 1572872 | tf_op jit(solution)/shard_map/ppermute | solution.py:25
  69.4 34.7 %all-to-all-start.1 = ((bf16[64,64,128]{2,1,0:T(8,128)(2,1)}), bf16[64,64,128]{2,1,0:T(8,128)(2,1)S(1)}, u32[]{:S(2)}, u32[]{:S(2)}) async-start(bf16[64,64,128]{2,1,0:T(8,128)(2,1)} %slice.76), calls=%async_computation.1 | async-start | bytes 2097152 | tf_op jit(solution)/shard_map/all_to_all | solution.py:191
  104.1 79.7 %all-to-all-start.2 = ((bf16[64,128,128]{2,1,0:T(8,128)(2,1)}), bf16[64,128,128]{2,1,0:T(8,128)(2,1)S(1)}, u32[]{:S(2)}, u32[]{:S(2)}) async-start(bf16[64,128,128]{2,1,0:T(8,128)(2,1)} %pad_maximum_fusion), calls=%async_computation.2 | async-start | bytes 4194304 | tf_op jit(solution)/shard_map/all_to_all | solution.py:191
  110.6 56.9 %copy-start.2 = (bf16[8,8,32,128]{3,1,2,0:T(8,128)(2,1)}, bf16[8,8,32,128]{3,1,2,0:T(8,128)(2,1)S(1)}, u32[]{:S(2)}) copy-start(bf16[8,8,32,128]{3,1,2,0:T(8,128)(2,1)S(1)} %copy.39) | copy-start | bytes 1572868
  110.8 56.7 %copy-start.3 = (bf16[8,8,32,128]{3,1,2,0:T(8,128)(2,1)}, bf16[8,8,32,128]{3,1,2,0:T(8,128)(2,1)S(1)}, u32[]{:S(2)}) copy-start(bf16[8,8,32,128]{3,1,2,0:T(8,128)(2,1)S(1)} %copy.38) | copy-start | bytes 1572868
  110.8 26.2 %collective-permute-start.3 = (bf16[64,4096]{1,0:T(8,128)(2,1)S(1)}, bf16[64,4096]{1,0:T(8,128)(2,1)S(1)}, u32[]{:S(2)}, u32[]{:S(2)}) collective-permute-start(bf16[64,4096]{1,0:T(8,128)(2,1)S(1)} %bitcast.64), channel_id=1, source_target_pairs={{0,1},{1,2},{2,3},{3,0},{4,5},{5,6},{6,7},{7,4},{8,9},{9,10},{10,1... | collective-permute-start | bytes 1572872 | tf_op jit(solution)/shard_map/ppermute | solution.py:25
  112.1 25.0 %collective-permute-start.6 = (bf16[64,4096]{1,0:T(8,128)(2,1)S(1)}, bf16[64,4096]{1,0:T(8,128)(2,1)S(1)}, u32[]{:S(2)}, u32[]{:S(2)}) collective-permute-start(bf16[64,4096]{1,0:T(8,128)(2,1)S(1)} %bitcast.68), channel_id=1, source_target_pairs={{0,3},{1,0},{2,1},{3,2},{4,7},{5,4},{6,5},{7,6},{8,11},{9,8},{10,9... | collective-permute-start | bytes 1572872 | tf_op jit(solution)/shard_map/ppermute | solution.py:25
  113.6 41.9 %collective-permute-start.4 = (bf16[64,4096]{1,0:T(8,128)(2,1)S(1)}, bf16[64,4096]{1,0:T(8,128)(2,1)S(1)}, u32[]{:S(2)}, u32[]{:S(2)}) collective-permute-start(bf16[64,4096]{1,0:T(8,128)(2,1)S(1)} %bitcast.69), channel_id=1, source_target_pairs={{0,1},{1,2},{2,3},{3,0},{4,5},{5,6},{6,7},{7,4},{8,9},{9,10},{10,1... | collective-permute-start | bytes 1572872 | tf_op jit(solution)/shard_map/ppermute | solution.py:25
  113.6 41.9 %collective-permute-start.5 = (bf16[64,4096]{1,0:T(8,128)(2,1)S(1)}, bf16[64,4096]{1,0:T(8,128)(2,1)S(1)}, u32[]{:S(2)}, u32[]{:S(2)}) collective-permute-start(bf16[64,4096]{1,0:T(8,128)(2,1)S(1)} %bitcast.65), channel_id=1, source_target_pairs={{0,3},{1,0},{2,1},{3,2},{4,7},{5,4},{6,5},{7,6},{8,11},{9,8},{10,9... | collective-permute-start | bytes 1572872 | tf_op jit(solution)/shard_map/ppermute | solution.py:25
  137.1 18.4 %copy-start.4 = (bf16[64,4096]{1,0:T(8,128)(2,1)}, bf16[64,4096]{1,0:T(8,128)(2,1)S(1)}, u32[]{:S(2)}) copy-start(bf16[64,4096]{1,0:T(8,128)(2,1)S(1)} %collective-permute-done.3.refs_4_) | copy-start | bytes 1572868
  137.1 29.6 %collective-permute-start.7 = (bf16[64,4096]{1,0:T(8,128)(2,1)S(1)}, bf16[64,4096]{1,0:T(8,128)(2,1)S(1)}, u32[]{:S(2)}, u32[]{:S(2)}) collective-permute-start(bf16[64,4096]{1,0:T(8,128)(2,1)S(1)} %collective-permute-done.3.refs_4_), channel_id=1, source_target_pairs={{0,1},{1,2},{2,3},{3,0},{4,5},{5,6},{6,7},{7,4},{8,9},{9,10},{10,1... | collective-permute-start | bytes 1572872 | tf_op jit(solution)/shard_map/ppermute | solution.py:25
  137.1 29.6 %copy-start.5 = (bf16[64,4096]{1,0:T(8,128)(2,1)}, bf16[64,4096]{1,0:T(8,128)(2,1)S(1)}, u32[]{:S(2)}) copy-start(bf16[64,4096]{1,0:T(8,128)(2,1)S(1)} %collective-permute-done.6.refs_7_) | copy-start | bytes 1572868
  137.1 30.4 %collective-permute-start.8 = (bf16[64,4096]{1,0:T(8,128)(2,1)S(1)}, bf16[64,4096]{1,0:T(8,128)(2,1)}, u32[]{:S(2)}, u32[]{:S(2)}) collective-permute-start(bf16[64,4096]{1,0:T(8,128)(2,1)S(1)} %collective-permute-done.6.refs_7_), channel_id=1, source_target_pairs={{0,3},{1,0},{2,1},{3,2},{4,7},{5,4},{6,5},{7,6},{8,11},{9,8},{10,9... | collective-permute-start | bytes 1572872 | tf_op jit(solution)/shard_map/ppermute | solution.py:25
  155.5 11.2 %copy-start.6 = (bf16[64,4096]{1,0:T(8,128)(2,1)}, bf16[64,4096]{1,0:T(8,128)(2,1)S(1)}, u32[]{:S(2)}) copy-start(bf16[64,4096]{1,0:T(8,128)(2,1)S(1)} %collective-permute-done.4.refs_5_) | copy-start | bytes 1572868
  155.5 11.2 %copy-start.7 = (bf16[64,4096]{1,0:T(8,128)(2,1)}, bf16[64,4096]{1,0:T(8,128)(2,1)S(1)}, u32[]{:S(2)}) copy-start(bf16[64,4096]{1,0:T(8,128)(2,1)S(1)} %collective-permute-done.5.refs_6_) | copy-start | bytes 1572868
  166.7 0.8 copy-start.8
  181.1 19.3 %collective-permute-start.13 = (bf16[64,4224]{1,0:T(8,128)(2,1)}, bf16[64,4224]{1,0:T(8,128)(2,1)S(1)}, u32[]{:S(2)}, u32[]{:S(2)}) collective-permute-start(bf16[64,4224]{1,0:T(8,128)(2,1)} %get-tuple-element.42), channel_id=1, source_target_pairs={{0,1},{1,2},{2,3},{3,0},{4,5},{5,6},{6,7},{7,4},{8,9},{9,10},{10,1... | collective-permute-start | bytes 1622024 | tf_op jit(solution)/shard_map/ppermute | solution.py:25
  181.2 20.4 %collective-permute-start.14 = (bf16[64,4224]{1,0:T(8,128)(2,1)}, bf16[64,4224]{1,0:T(8,128)(2,1)S(1)}, u32[]{:S(2)}, u32[]{:S(2)}) collective-permute-start(bf16[64,4224]{1,0:T(8,128)(2,1)} %get-tuple-element.43), channel_id=1, source_target_pairs={{0,3},{1,0},{2,1},{3,2},{4,7},{5,4},{6,5},{7,6},{8,11},{9,8},{10,9... | collective-permute-start | bytes 1622024 | tf_op jit(solution)/shard_map/ppermute | solution.py:25
  188.3 12.1 %copy-start.17 = (bf16[64,4224]{1,0:T(8,128)(2,1)S(1)}, bf16[64,4224]{1,0:T(8,128)(2,1)}, u32[]{:S(2)}) copy-start(bf16[64,4224]{1,0:T(8,128)(2,1)} %get-tuple-element.49) | copy-start | bytes 1622020
  188.3 13.4 %copy-start.11 = (bf16[64,4224]{1,0:T(8,128)(2,1)S(1)}, bf16[64,4224]{1,0:T(8,128)(2,1)}, u32[]{:S(2)}) copy-start(bf16[64,4224]{1,0:T(8,128)(2,1)} %get-tuple-element.47) | copy-start | bytes 1622020
  197.6 4.5 %copy-start.10 = (bf16[64,4224]{1,0:T(8,128)(2,1)S(1)}, bf16[64,4224]{1,0:T(8,128)(2,1)}, u32[]{:S(2)}) copy-start(bf16[64,4224]{1,0:T(8,128)(2,1)} %get-tuple-element.41) | copy-start | bytes 1622020
  197.6 64.7 %collective-permute-start.11 = (bf16[64,4224]{1,0:T(8,128)(2,1)}, bf16[64,4224]{1,0:T(8,128)(2,1)}, u32[]{:S(2)}, u32[]{:S(2)}) collective-permute-start(bf16[64,4224]{1,0:T(8,128)(2,1)} %get-tuple-element.38), channel_id=1, source_target_pairs={{0,1},{1,2},{2,3},{3,0},{4,5},{5,6},{6,7},{7,4},{8,9},{9,10},{10,1... | collective-permute-start | bytes 1622024 | tf_op jit(solution)/shard_map/ppermute | solution.py:25
  197.7 64.6 %collective-permute-start.10 = (bf16[64,4224]{1,0:T(8,128)(2,1)}, bf16[64,4224]{1,0:T(8,128)(2,1)}, u32[]{:S(2)}, u32[]{:S(2)}) collective-permute-start(bf16[64,4224]{1,0:T(8,128)(2,1)} %get-tuple-element.37), channel_id=1, source_target_pairs={{0,3},{1,0},{2,1},{3,2},{4,7},{5,4},{6,5},{7,6},{8,11},{9,8},{10,9... | collective-permute-start | bytes 1622024 | tf_op jit(solution)/shard_map/ppermute | solution.py:25
  200.4 61.9 %collective-permute-start.9 = (bf16[64,4224]{1,0:T(8,128)(2,1)}, bf16[64,4224]{1,0:T(8,128)(2,1)}, u32[]{:S(2)}, u32[]{:S(2)}) collective-permute-start(bf16[64,4224]{1,0:T(8,128)(2,1)} %get-tuple-element.36), channel_id=1, source_target_pairs={{0,2},{1,3},{2,0},{3,1},{4,6},{5,7},{6,4},{7,5},{8,10},{9,11},{10,... | collective-permute-start | bytes 1622024 | tf_op jit(solution)/shard_map/ppermute | solution.py:25
  200.4 33.4 %collective-permute-start.17 = (bf16[64,4224]{1,0:T(8,128)(2,1)S(1)}, bf16[64,4224]{1,0:T(8,128)(2,1)S(1)}, u32[]{:S(2)}, u32[]{:S(2)}) collective-permute-start(bf16[64,4224]{1,0:T(8,128)(2,1)S(1)} %copy-done.17), channel_id=1, source_target_pairs={{0,3},{1,0},{2,1},{3,2},{4,7},{5,4},{6,5},{7,6},{8,11},{9,8},{10,9... | collective-permute-start | bytes 1622024 | tf_op jit(solution)/shard_map/ppermute | solution.py:25
  201.7 32.1 %copy-start.16 = (bf16[64,4224]{1,0:T(8,128)(2,1)S(1)}, bf16[64,4224]{1,0:T(8,128)(2,1)}, u32[]{:S(2)}) copy-start(bf16[64,4224]{1,0:T(8,128)(2,1)} %get-tuple-element.40) | copy-start | bytes 1622020
  201.7 35.6 %copy-start.14 = (bf16[64,4224]{1,0:T(8,128)(2,1)S(1)}, bf16[64,4224]{1,0:T(8,128)(2,1)}, u32[]{:S(2)}) copy-start(bf16[64,4224]{1,0:T(8,128)(2,1)} %get-tuple-element.46) | copy-start | bytes 1622020
  201.8 33.0 %collective-permute-start.16 = (bf16[64,4224]{1,0:T(8,128)(2,1)S(1)}, bf16[64,4224]{1,0:T(8,128)(2,1)S(1)}, u32[]{:S(2)}, u32[]{:S(2)}) collective-permute-start(bf16[64,4224]{1,0:T(8,128)(2,1)S(1)} %add_convert_fusion.1), channel_id=1, source_target_pairs={{0,1},{1,2},{2,3},{3,0},{4,5},{5,6},{6,7},{7,4},{8,9},{9,10},{10,1... | collective-permute-start | bytes 1622024 | tf_op jit(solution)/shard_map/ppermute | solution.py:25
  202.2 45.2 %copy-start.12 = (bf16[64,4224]{1,0:T(8,128)(2,1)S(1)}, bf16[64,4224]{1,0:T(8,128)(2,1)}, u32[]{:S(2)}) copy-start(bf16[64,4224]{1,0:T(8,128)(2,1)} %get-tuple-element.39) | copy-start | bytes 1622020
  233.8 13.5 %collective-permute-start.12 = (bf16[64,4224]{1,0:T(8,128)(2,1)S(1)}, bf16[64,4224]{1,0:T(8,128)(2,1)S(1)}, u32[]{:S(2)}, u32[]{:S(2)}) collective-permute-start(bf16[64,4224]{1,0:T(8,128)(2,1)S(1)} %copy-done.16), channel_id=1, source_target_pairs={{0,1},{1,2},{2,3},{3,0},{4,5},{5,6},{6,7},{7,4},{8,9},{9,10},{10,1... | collective-permute-start | bytes 1622024 | tf_op jit(solution)/shard_map/ppermute | solution.py:25
  234.8 12.5 %collective-permute-start.15 = (bf16[64,4224]{1,0:T(8,128)(2,1)S(1)}, bf16[64,4224]{1,0:T(8,128)(2,1)S(1)}, u32[]{:S(2)}, u32[]{:S(2)}) collective-permute-start(bf16[64,4224]{1,0:T(8,128)(2,1)S(1)} %add_convert_fusion.3), channel_id=1, source_target_pairs={{0,3},{1,0},{2,1},{3,2},{4,7},{5,4},{6,5},{7,6},{8,11},{9,8},{10,9... | collective-permute-start | bytes 1622024 | tf_op jit(solution)/shard_map/ppermute | solution.py:25
  249.0 13.4 %copy-start.13 = (bf16[64,4224]{1,0:T(8,128)(2,1)S(1)}, bf16[64,4224]{1,0:T(8,128)(2,1)}, u32[]{:S(2)}) copy-start(bf16[64,4224]{1,0:T(8,128)(2,1)} %get-tuple-element.35) | copy-start | bytes 1622020
  249.0 41.9 %all-to-all-start.3 = ((bf16[64,64,128]{2,1,0:T(8,128)(2,1)}), bf16[64,64,128]{2,1,0:T(8,128)(2,1)S(1)}, u32[]{:S(2)}, u32[]{:S(2)}) async-start(bf16[64,64,128]{2,1,0:T(8,128)(2,1)} %bitcast.27), calls=%async_computation.3 | async-start | bytes 2097152 | tf_op jit(solution)/shard_map/all_to_all | solution.py:191
  292.0 26.4 %all-to-all-start.4 = ((bf16[64,35,128]{2,1,0:T(8,128)(2,1)}), bf16[64,35,128]{2,1,0:T(8,128)(2,1)}, u32[]{:S(2)}, u32[]{:S(2)}) async-start(bf16[64,35,128]{2,1,0:T(8,128)(2,1)} %reshape.84), calls=%async_computation.4 | async-start | bytes 1310720 | tf_op jit(solution)/shard_map/all_to_all | solution.py:191
  320.1 2.2 copy-start.1
Sparse Core Ops, SparseCore 0:
  68.4 82.9 all-gather.1
